TPU v7x, 32 devices: a whole 2x2x4 slice. The times are simulated.
32 devices in a mesh: dp: 16 (over z, y, x), mp: 2 (over core).
Axes of the slice: x: 2, y: 2, z: 4, core: 2. Of those that a mesh axis runs over, the one named last changes fastest.
Arguments:
- hidden: bfloat16 [2048, 4096], P('dp', 'mp'), may hold values from -6 to 6
- attended: bfloat16 [2048, 4096], P('dp', 'mp'), may hold values from -6 to 6
- query_cotangent: bfloat16 [2048, 4096], P('dp', 'mp'), may hold values from -1.5 to 1.5
- output_cotangent: bfloat16 [2048, 4096], P('dp', 'mp'), may hold values from -1.5 to 1.5
- query_projection_weight: bfloat16 [4096, 4096], P('dp', 'mp'), may hold values from -0.09375 to 0.09375
- output_projection_weight: bfloat16 [4096, 4096], P('dp', 'mp'), may hold values from -0.09375 to 0.09375
- narrower: bfloat16 [256, 16, 4096], P('dp', None, 'mp'), may hold values from -0.09375 to 0.09375
- widener: bfloat16 [256, 16, 4096], P('dp', None, 'mp'), may hold values from -0.375 to 0.375
- reducer: bfloat16 [256, 16, 4096], P('dp', None, 'mp'), may hold values from -0.09375 to 0.09375
- enlarger: bfloat16 [256, 16, 4096], P('dp', None, 'mp'), may hold values from -0.375 to 0.375
- block_adapter: int32 [512], P('dp'), may hold values from 0 to 255, as said below
- block_fill: int32 [512], P('dp'), may hold values from 1 to 4
Outputs:
- queries: bfloat16 [2048, 4096], P('dp', 'mp')
- projected: bfloat16 [2048, 4096], P('dp', 'mp')
- hidden_state_gradient: bfloat16 [2048, 4096], P('dp', 'mp')
- attention_output_gradient: bfloat16 [2048, 4096], P('dp', 'mp')
- narrower_gradient: float32 [256, 16, 4096], P('dp', None, 'mp')
- widener_gradient: float32 [256, 16, 4096], P('dp', None, 'mp')
- reducer_gradient: float32 [256, 16, 4096], P('dp', None, 'mp')
- enlarger_gradient: float32 [256, 16, 4096], P('dp', None, 'mp')
Inputs may be any that keep to these rules, and one draw needn't show every extreme that they name: `block_adapter`: the owner of adapter e is e // 16. Among the 32 blocks of one group (one index of dp), at most 2 have adapters of one owner, and some owner has exactly 2 blocks in every group.
All inputs are finite; a program needn't handle non-finite values.
Results may differ from a plain program's by a relative error of at most 0.015.
Values may be sent and summed in bfloat16 or wider, within the bound.
A program may use at most 128 MiB of HBM per device.

v0:
```python
import jax
import jax.numpy as jnp
from jax import lax
from jax.sharding import Mesh, PartitionSpec as P

adapter_scale = 2.0


def product(left, right, contract):
    return lax.dot_general(
        left, right, ((contract[:1], contract[1:]), ((), ())), preferred_element_type=jnp.float32
    )


def one_hot(condition):
    return condition.astype(jnp.bfloat16)


def iota(shape, dimension):
    return lax.broadcasted_iota(jnp.int32, shape, dimension)


def stacked_columns(values, parts):
    wide = values.shape[1] // parts
    return jnp.concatenate([values[:, i * wide : (i + 1) * wide] for i in range(parts)], axis=0)


def unstacked_columns(values, parts):
    rows = values.shape[0] // parts
    return jnp.concatenate([values[i * rows : (i + 1) * rows] for i in range(parts)], axis=1)


def exchange(values, axis):
    return lax.all_to_all(values, axis, split_axis=0, concat_axis=0, tiled=True)


def on_device(
    hidden,
    attended,
    query_cotangent,
    output_cotangent,
    query_projection_weight,
    output_projection_weight,
    narrower,
    widener,
    reducer,
    enlarger,
    block_adapter,
    block_fill,
):
    dp = ("far", "near")
    far = lax.axis_size("far")
    owners = far * lax.axis_size("near")
    tokens = hidden.shape[0]
    group_blocks = block_adapter.shape[0]
    width = tokens // group_blocks
    capacity = -(-group_blocks // owners)
    per_owner, rank = narrower.shape[:2]
    lanes = -(-per_owner // 128) * 128
    query_rows = lax.all_gather(query_projection_weight, "near", axis=0, tiled=True)
    output_rows = lax.all_gather(output_projection_weight, "near", axis=0, tiled=True)
    row_ids = iota((group_blocks, width), 1)
    live = one_hot(row_ids < block_fill[:, None]).reshape(tokens, 1)
    query_masked = query_cotangent * live
    output_masked = output_cotangent * live
    owner_of = block_adapter // per_owner
    later_ids = iota((group_blocks, group_blocks), 0)
    earlier_ids = iota((group_blocks, group_blocks), 1)
    before = (owner_of[:, None] == owner_of[None, :]) & (earlier_ids < later_ids)
    position = jnp.sum(before.astype(jnp.int32), axis=1)
    slot_of = owner_of * capacity + position
    row_of = (slot_of[:, None] * width + row_ids).reshape(1, tokens)
    table = one_hot(iota((owners * capacity * width, tokens), 0) == row_of)
    local_of = jnp.broadcast_to((block_adapter % per_owner)[:, None], (group_blocks, width))
    local_hot = one_hot(iota((tokens, lanes), 1) == local_of.reshape(tokens, 1))
    sent = jnp.concatenate(
        [
            product(table, part, (1, 0)).astype(jnp.bfloat16)
            for part in (local_hot, hidden, attended, query_masked, output_masked)
        ],
        axis=1,
    )
    received = exchange(sent, dp)
    model, query = (hidden.shape[1], attended.shape[1])
    ends = [lanes, lanes + model, lanes + model + query, lanes + model + 2 * query]
    hot, hid, att, qcot, ocot = jnp.split(received, ends, axis=1)
    many = per_owner * rank
    spread = one_hot(iota((lanes, many), 0) == iota((lanes, many), 1) // rank)
    own = product(hot, spread, (1, 0))
    fold = one_hot(iota((many, rank), 0) % rank == iota((many, rank), 1))
    factors = [f.reshape(many, f.shape[2]) for f in (narrower, reducer, widener, enlarger)]
    folded = jnp.concatenate(
        [
            product((product(x, f, (1, 1)) * own).astype(jnp.bfloat16), fold, (1, 0))
            for x, f in zip((hid, att, qcot, ocot), factors)
        ],
        axis=1,
    ).astype(jnp.bfloat16)
    ranks = lax.psum(folded, "mp")
    query_rank, output_rank, query_back, output_back = [
        (product(ranks[:, i * rank : (i + 1) * rank], fold, (1, 1)) * own).astype(jnp.bfloat16)
        for i in range(4)
    ]
    down_query, down_output, up_query, up_output = factors
    returned = exchange(
        jnp.concatenate(
            [
                (adapter_scale * product(r, f, (1, 0))).astype(jnp.bfloat16)
                for r, f in (
                    (query_rank, up_query),
                    (output_rank, up_output),
                    (query_back, down_query),
                    (output_back, down_output),
                )
            ],
            axis=1,
        ),
        dp,
    )

    def gradient(ranks, rows, like):
        return (adapter_scale * product(ranks, rows, (0, 0))).reshape(like.shape)

    narrower_gradient = gradient(query_back, hid, narrower)
    widener_gradient = gradient(query_rank, qcot, widener)
    reducer_gradient = gradient(output_back, att, reducer)
    enlarger_gradient = gradient(output_rank, ocot, enlarger)
    hid_full = lax.all_gather(hidden, "mp", axis=1, tiled=True)
    att_full = lax.all_gather(attended, "mp", axis=1, tiled=True)
    depth = hid_full.shape[1] // far
    inputs = exchange(
        jnp.concatenate([stacked_columns(hid_full, far), stacked_columns(att_full, far)], axis=1),
        "far",
    )
    cotangents = [
        lax.all_gather(masked, "far", axis=0, tiled=True)
        for masked in (query_masked, output_masked)
    ]

    def forward(values, weight):
        part = product(values, weight, (1, 0)).astype(jnp.bfloat16)
        parts = exchange(part, "far").reshape(far, tokens, weight.shape[1])
        return jnp.sum(parts.astype(jnp.float32), axis=0)

    def backward(masked, weight):
        part = product(masked, weight, (1, 1)).astype(jnp.bfloat16)
        whole = unstacked_columns(exchange(part, "far"), far)
        return lax.psum_scatter(whole, "mp", scatter_dimension=1, tiled=True)

    base = [
        forward(inputs[:, :depth], query_rows),
        forward(inputs[:, depth:], output_rows),
        backward(cotangents[0], query_rows).astype(jnp.float32),
        backward(cotangents[1], output_rows).astype(jnp.float32),
    ]
    starts = [query, query + model, query + 2 * model]
    adapter_terms = [product(table, part, (0, 0)) for part in jnp.split(returned, starts, axis=1)]
    queries, projected, hidden_state_gradient, attention_output_gradient = [
        (b + t).astype(jnp.bfloat16) for b, t in zip(base, adapter_terms)
    ]
    return (
        queries,
        projected,
        hidden_state_gradient,
        attention_output_gradient,
        narrower_gradient,
        widener_gradient,
        reducer_gradient,
        enlarger_gradient,
    )


def solution(mesh):
    count = mesh.shape["dp"]
    far = 1
    while far * far < count or count % far:
        far += 1
    split = Mesh(mesh.devices.reshape(far, count // far, mesh.shape["mp"]), ("far", "near", "mp"))
    dp = ("far", "near")
    rows, factors = (P(dp, "mp"), P(dp, None, "mp"))
    return jax.shard_map(
        on_device,
        mesh=split,
        in_specs=(rows,) * 6 + (factors,) * 4 + (P(dp),) * 2,
        out_specs=(rows,) * 4 + (factors,) * 4,
        check_vma=False,
    )
```

profile of v0, /device:TPU:12, one launch (start us, length us, event | category | flops | bytes accessed | tf_op | source)
XLA Modules:
  0.0 492.3 jit_solution(7176359094371279426)
XLA Ops:
  9.6 2.4 broadcast_multiply_fusion
  16.8 7.2 %all-to-all-start.2 = ((bf16[16,8,8320]{2,1,0:T(8,128)(2,1)}), bf16[16,8,8320]{2,1,0:T(8,128)(2,1)S(1)}, u32[]{:S(2)}, u32[]{:S(2)}) async-start(bf16[16,8,8320]{2,1,0:T(8,128)(2,1)} %bitcast.73), calls=%async_computation.2 | async-start | bytes 4259840 | tf_op jit(solution)/shard_map/all_to_all | solution.py:34
  26.6 5.1 %all-gather.9.cloned.1.call-done = bf16[128,4096]{1,0:T(8,128)(2,1)} async-done(((bf16[128,2048]{1,0:T(8,128)(2,1)}), bf16[128,4096]{1,0:T(8,128)(2,1)}) %all-gather.9.cloned.1.call-update) | async-done | bytes 1048592 | tf_op jit(solution)/shard_map/all_gather | solution.py:129
  33.2 13.9 %maximum_maximum_fusion = bf16[512,2048]{1,0:T(8,128)(2,1)} fusion(bf16[128,1024]{1,0:T(8,128)(2,1)S(1)} %get-tuple-element.21, bf16[128,1024]{1,0:T(8,128)(2,1)S(1)} %get-tuple-element.22, bf16[128,1024]{1,0:T(8,128)(2,1)S(1)} %get-tuple-element.23, bf16[128,1024]{1,0:T(8,128)(2,1)S(1)} %get-tuple-element.20, bf16[128,1024]{1,0:T(8,128)(2,1)S(1)} %copy-done.9, ...), kind=kLoop, calls=%fused_computation.32 | loop fusion | flops 16777216 | bytes 4194304 | tf_op jit(solution)/shard_map/concatenate | solution.py:132
  47.1 59.3 %all-to-all-done.2 = bf16[16,8,8320]{2,1,0:T(8,128)(2,1)S(1)} async-done(((bf16[16,8,8320]{2,1,0:T(8,128)(2,1)}), bf16[16,8,8320]{2,1,0:T(8,128)(2,1)S(1)}, u32[]{:S(2)}, u32[]{:S(2)}) %all-to-all-start.2) | async-done | bytes 2129952 | tf_op jit(solution)/shard_map/all_to_all | solution.py:34
  106.4 4.5 all-to-all-start
  110.9 48.8 %all-gather.11.cloned.1.call-done = bf16[1024,2048]{1,0:T(8,128)(2,1)} async-done(((bf16[256,2048]{1,0:T(8,128)(2,1)}), bf16[1024,2048]{1,0:T(8,128)(2,1)}) %all-gather.11.cloned.1.call-update) | async-done | bytes 4194320 | tf_op jit(solution)/shard_map/all_gather | solution.py:60
  159.7 6.2 %convolution_convert_fusion.7 = bf16[512,1024]{1,0:T(8,128)(2,1)} fusion(bf16[512,2048]{1,0:T(8,128)(2,1)} %all-gather.15.cloned.1.call-done, bf16[1024,2048]{1,0:T(8,128)(2,1)} %all-gather.11.cloned.1.call-done), kind=kOutput, calls=%fused_computation.35 | convolution fusion | flops 2148007936 | bytes 7340032 | tf_op jit(solution)/shard_map/dot_general | solution.py:10
  165.9 5.1 %all-to-all-start.5 = ((bf16[4,128,1024]{2,1,0:T(8,128)(2,1)}), bf16[4,128,1024]{2,1,0:T(8,128)(2,1)}, u32[]{:S(2)}, u32[]{:S(2)}) async-start(bf16[4,128,1024]{2,1,0:T(8,128)(2,1)} %bitcast.86), calls=%async_computation.5 | async-start | bytes 2097152 | tf_op jit(solution)/shard_map/all_to_all | solution.py:34
  171.0 56.3 %all-gather.17.cloned.1.call-done = bf16[512,2048]{1,0:T(8,128)(2,1)} async-done(((bf16[128,2048]{1,0:T(8,128)(2,1)}), bf16[512,2048]{1,0:T(8,128)(2,1)}) %all-gather.17.cloned.1.call-update) | async-done | bytes 2097168 | tf_op jit(solution)/shard_map/all_gather | solution.py:136
  227.3 55.3 %all-gather.13.cloned.1.call-done = bf16[1024,2048]{1,0:T(8,128)(2,1)} async-done(((bf16[256,2048]{1,0:T(8,128)(2,1)}), bf16[1024,2048]{1,0:T(8,128)(2,1)}) %all-gather.13.cloned.1.call-update) | async-done | bytes 4194320 | tf_op jit(solution)/shard_map/all_gather | solution.py:61
  282.6 6.2 %convolution_convert_fusion.6 = bf16[512,1024]{1,0:T(8,128)(2,1)} fusion(bf16[512,2048]{1,0:T(8,128)(2,1)} %all-gather.17.cloned.1.call-done, bf16[1024,2048]{1,0:T(8,128)(2,1)} %all-gather.13.cloned.1.call-done), kind=kOutput, calls=%fused_computation.34 | convolution fusion | flops 2148007936 | bytes 7340032 | tf_op jit(solution)/shard_map/dot_general | solution.py:10
  288.8 5.1 %all-to-all-start.6 = ((bf16[4,128,1024]{2,1,0:T(8,128)(2,1)}), bf16[4,128,1024]{2,1,0:T(8,128)(2,1)}, u32[]{:S(2)}, u32[]{:S(2)}) async-start(bf16[4,128,1024]{2,1,0:T(8,128)(2,1)} %bitcast.87), calls=%async_computation.7 | async-start | bytes 2097152 | tf_op jit(solution)/shard_map/all_to_all | solution.py:34
  293.9 6.2 %convolution_convert_fusion = bf16[512,2048]{1,0:T(8,128)(2,1)} fusion(bf16[1024,2048]{1,0:T(8,128)(2,1)} %all-gather.13.cloned.1.call-done, bf16[512,2048]{1,0:T(8,128)(2,1)} %bitcast.1), kind=kOutput, calls=%fused_computation.2 | convolution fusion | flops 2148532224 | bytes 7340032 | tf_op jit(solution)/shard_map/dot_general | solution.py:10
  300.1 16.1 %all-to-all-done.6 = bf16[4,128,1024]{2,1,0:T(8,128)(2,1)} async-done(((bf16[4,128,1024]{2,1,0:T(8,128)(2,1)}), bf16[4,128,1024]{2,1,0:T(8,128)(2,1)}, u32[]{:S(2)}, u32[]{:S(2)}) %all-to-all-start.6) | async-done | bytes 1048608 | tf_op jit(solution)/shard_map/all_to_all | solution.py:34
  316.2 7.8 %all-to-all-start.4 = ((bf16[4,128,2048]{2,1,0:T(8,128)(2,1)}), bf16[4,128,2048]{2,1,0:T(8,128)(2,1)}, u32[]{:S(2)}, u32[]{:S(2)}) async-start(bf16[4,128,2048]{2,1,0:T(8,128)(2,1)} %bitcast.79), calls=%async_computation.4 | async-start | bytes 4194304 | tf_op jit(solution)/shard_map/all_to_all | solution.py:34
  328.4 6.2 %convolution_convert_fusion.1 = bf16[512,2048]{1,0:T(8,128)(2,1)} fusion(bf16[1024,2048]{1,0:T(8,128)(2,1)} %all-gather.11.cloned.1.call-done, bf16[512,2048]{1,0:T(8,128)(2,1)} %bitcast.1), kind=kOutput, calls=%fused_computation.3 | convolution fusion | flops 2148532224 | bytes 7340032 | tf_op jit(solution)/shard_map/dot_general | solution.py:10
  334.6 33.9 %all-to-all-done.4 = bf16[4,128,2048]{2,1,0:T(8,128)(2,1)} async-done(((bf16[4,128,2048]{2,1,0:T(8,128)(2,1)}), bf16[4,128,2048]{2,1,0:T(8,128)(2,1)}, u32[]{:S(2)}, u32[]{:S(2)}) %all-to-all-start.4) | async-done | bytes 2097184 | tf_op jit(solution)/shard_map/all_to_all | solution.py:34
  368.4 7.8 %all-to-all-start.1 = ((bf16[4,128,2048]{2,1,0:T(8,128)(2,1)}), bf16[4,128,2048]{2,1,0:T(8,128)(2,1)}, u32[]{:S(2)}, u32[]{:S(2)}) async-start(bf16[4,128,2048]{2,1,0:T(8,128)(2,1)} %bitcast.78), calls=%async_computation.1 | async-start | bytes 4194304 | tf_op jit(solution)/shard_map/all_to_all | solution.py:34
  378.1 3.4 psum.7
  385.9 34.8 %all-to-all-done.1 = bf16[4,128,2048]{2,1,0:T(8,128)(2,1)} async-done(((bf16[4,128,2048]{2,1,0:T(8,128)(2,1)}), bf16[4,128,2048]{2,1,0:T(8,128)(2,1)}, u32[]{:S(2)}, u32[]{:S(2)}) %all-to-all-start.1) | async-done | bytes 2097184 | tf_op jit(solution)/shard_map/all_to_all | solution.py:34
  420.7 7.6 %all-to-all-start.3 = ((bf16[16,8,8192]{2,1,0:T(8,128)(2,1)}), bf16[16,8,8192]{2,1,0:T(8,128)(2,1)}, u32[]{:S(2)}, u32[]{:S(2)}) async-start(bf16[16,8,8192]{2,1,0:T(8,128)(2,1)} %maximum_bitcast_fusion), calls=%async_computation.3 | async-start | bytes 4194304 | tf_op jit(solution)/shard_map/all_to_all | solution.py:34
  444.6 31.7 %all-to-all-done.3 = bf16[16,8,8192]{2,1,0:T(8,128)(2,1)} async-done(((bf16[16,8,8192]{2,1,0:T(8,128)(2,1)}), bf16[16,8,8192]{2,1,0:T(8,128)(2,1)}, u32[]{:S(2)}, u32[]{:S(2)}) %all-to-all-start.3) | async-done | bytes 2097184 | tf_op jit(solution)/shard_map/all_to_all | solution.py:34
  483.1 2.3 fusion.6
  (102 shorter events, 44.7 us)
Async XLA Ops:
  7.2 318.8 %copy-start = (bf16[16,16,2048]{2,1,0:T(8,128)(2,1)S(1)}, bf16[16,16,2048]{2,1,0:T(8,128)(2,1)}, u32[]{:S(2)}) copy-start(bf16[16,16,2048]{2,1,0:T(8,128)(2,1)} %param.19) | copy-start | bytes 3145732
  7.2 17.3 %all-gather.7.cloned.1.call-start = ((), (), s32[]{:S(2)}) async-start(), calls=%async_computation.9 | async-start | bytes 1572864 | tf_op jit(solution)/shard_map/all_gather | solution.py:128
  7.9 23.8 %all-gather.9.cloned.1.call-start = ((), (), s32[]{:S(2)}) async-start(), calls=%async_computation.10 | async-start | bytes 1572864 | tf_op jit(solution)/shard_map/all_gather | solution.py:129
  8.7 4.5 copy-start.14
  8.7 102.2 %all-gather.15.cloned.1.call-start = ((), (), s32[]{:S(2)}) async-start(), calls=%async_computation.13 | async-start | bytes 2621440 | tf_op jit(solution)/shard_map/all_gather | solution.py:136
  9.6 4.6 copy-start.4
  11.9 2.5 copy-start.5
  11.9 2.8 copy-start.2
  12.0 147.7 %all-gather.11.cloned.1.call-start = ((), (), s32[]{:S(2)}) async-start(), calls=%async_computation.11 | async-start | bytes 5242880 | tf_op jit(solution)/shard_map/all_gather | solution.py:60
  12.5 2.5 copy-start.1
  12.6 214.8 %all-gather.17.cloned.1.call-start = ((), (), s32[]{:S(2)}) async-start(), calls=%async_computation.15 | async-start | bytes 2621440 | tf_op jit(solution)/shard_map/all_gather | solution.py:136
  16.8 89.7 %all-to-all-start.2 = ((bf16[16,8,8320]{2,1,0:T(8,128)(2,1)}), bf16[16,8,8320]{2,1,0:T(8,128)(2,1)S(1)}, u32[]{:S(2)}, u32[]{:S(2)}) async-start(bf16[16,8,8320]{2,1,0:T(8,128)(2,1)} %bitcast.73), calls=%async_computation.2 | async-start | bytes 4259840 | tf_op jit(solution)/shard_map/all_to_all | solution.py:34
  23.9 258.7 %all-gather.13.cloned.1.call-start = ((), (), s32[]{:S(2)}) async-start(), calls=%async_computation.12 | async-start | bytes 5242880 | tf_op jit(solution)/shard_map/all_gather | solution.py:61
  106.4 59.4 %all-to-all-start = ((bf16[4,128,2048]{2,1,0:T(8,128)(2,1)}), bf16[4,128,2048]{2,1,0:T(8,128)(2,1)}, u32[]{:S(2)}, u32[]{:S(2)}) async-start(bf16[4,128,2048]{2,1,0:T(8,128)(2,1)} %bitcast.72), calls=%async_computation | async-start | bytes 4194304 | tf_op jit(solution)/shard_map/all_to_all | solution.py:34
  165.9 122.9 %all-to-all-start.5 = ((bf16[4,128,1024]{2,1,0:T(8,128)(2,1)}), bf16[4,128,1024]{2,1,0:T(8,128)(2,1)}, u32[]{:S(2)}, u32[]{:S(2)}) async-start(bf16[4,128,1024]{2,1,0:T(8,128)(2,1)} %bitcast.86), calls=%async_computation.5 | async-start | bytes 2097152 | tf_op jit(solution)/shard_map/all_to_all | solution.py:34
  288.8 27.4 %all-to-all-start.6 = ((bf16[4,128,1024]{2,1,0:T(8,128)(2,1)}), bf16[4,128,1024]{2,1,0:T(8,128)(2,1)}, u32[]{:S(2)}, u32[]{:S(2)}) async-start(bf16[4,128,1024]{2,1,0:T(8,128)(2,1)} %bitcast.87), calls=%async_computation.7 | async-start | bytes 2097152 | tf_op jit(solution)/shard_map/all_to_all | solution.py:34
  316.2 52.3 %all-to-all-start.4 = ((bf16[4,128,2048]{2,1,0:T(8,128)(2,1)}), bf16[4,128,2048]{2,1,0:T(8,128)(2,1)}, u32[]{:S(2)}, u32[]{:S(2)}) async-start(bf16[4,128,2048]{2,1,0:T(8,128)(2,1)} %bitcast.79), calls=%async_computation.4 | async-start | bytes 4194304 | tf_op jit(solution)/shard_map/all_to_all | solution.py:34
  368.4 52.3 %all-to-all-start.1 = ((bf16[4,128,2048]{2,1,0:T(8,128)(2,1)}), bf16[4,128,2048]{2,1,0:T(8,128)(2,1)}, u32[]{:S(2)}, u32[]{:S(2)}) async-start(bf16[4,128,2048]{2,1,0:T(8,128)(2,1)} %bitcast.78), calls=%async_computation.1 | async-start | bytes 4194304 | tf_op jit(solution)/shard_map/all_to_all | solution.py:34
  381.4 2.0 copy-start.7
  381.8 2.0 copy-start.12
  420.7 55.6 %all-to-all-start.3 = ((bf16[16,8,8192]{2,1,0:T(8,128)(2,1)}), bf16[16,8,8192]{2,1,0:T(8,128)(2,1)}, u32[]{:S(2)}, u32[]{:S(2)}) async-start(bf16[16,8,8192]{2,1,0:T(8,128)(2,1)} %maximum_bitcast_fusion), calls=%async_computation.3 | async-start | bytes 4194304 | tf_op jit(solution)/shard_map/all_to_all | solution.py:34
  428.3 2.7 copy-start.13
  428.3 52.4 %reduce-scatter.5.cloned.1.call-start = ((), (), s32[]{:S(2)}) async-start(), calls=%async_computation.16 | async-start | bytes 1572864 | tf_op jit(solution)/shard_map/reduce_scatter | solution.py:148
  430.7 52.4 %reduce-scatter.3.cloned.1.call-start = ((), (), s32[]{:S(2)}) async-start(), calls=%async_computation.14 | async-start | bytes 1572864 | tf_op jit(solution)/shard_map/reduce_scatter | solution.py:148
  (6 other events, 8.4 us)
Sparse Core Ops, SparseCore 0:
  9.5 10.3 all-gather.6
  21.5 10.1 all-gather.8
  33.9 69.3 all-gather.14
  105.0 54.6 all-gather.10
  161.7 65.5 all-gather.16
  229.0 53.5 all-gather.12
  431.4 9.5 reduce-scatter.4
  443.2 9.5 reduce-scatter.2
where the time goes:
time: 493 us; the launch traced here: 492 us
  waiting for transfers between devices  344 us (70%)
  matrix products  51 us (10%)
  starting transfers between devices  45.6 us (9%)
  other arithmetic  25.2 us (5%)
  between operations  14.5 us (3%)
  local copies, waits for them, and re-layouts  8.27 us (2%)
    all_to_all x7, waiting for transfers between devices, exchange(): return lax.all_to_all(values, axis, split_axis=0, concat_axis=0, tiled=True)  176 us
    all_gather x2, waiting for transfers between devices, on_device(): lax.all_gather(masked, 'far', axis=0, tiled=True)  56.3 us
    all_gather x1, waiting for transfers between devices, on_device(): lax.all_gather(output_projection_weight, 'near', axis=0, tiled=True)  55.3 us
    dot_general x30, matrix products, product(): lax.dot_general(left, right, ((contract[:1], contract[1:]), ((), ())), pr...  51 us
    all_gather x1, waiting for transfers between devices, on_device(): lax.all_gather(query_projection_weight, 'near', axis=0, tiled=True)  48.8 us
    all_to_all x7, starting transfers between devices, exchange(): return lax.all_to_all(values, axis, split_axis=0, concat_axis=0, tiled=True)  45 us
    concatenate x1, other arithmetic, on_device(): jnp.concatenate([stacked_columns(hid_full, far), stacked_columns(att_full...  13.9 us
  transfers between devices with their start and end apart: 15, of which 9 were waited for; matrix products, arithmetic and copies ran while one was open for 16% of the time, Pallas kernels for 0%

commit v1 on v0

--- a/solution.py
+++ b/solution.py
@@ -57,8 +57,14 @@
     capacity = -(-group_blocks // owners)
     per_owner, rank = narrower.shape[:2]
     lanes = -(-per_owner // 128) * 128
-    query_rows = lax.all_gather(query_projection_weight, "near", axis=0, tiled=True)
-    output_rows = lax.all_gather(output_projection_weight, "near", axis=0, tiled=True)
+    draft_the_tasks = lambda block_here, state: jnp.split(
+        lax.all_gather(jnp.concatenate([block_here, state], axis=1), "near", axis=0, tiled=True),
+        [block_here.shape[1]],
+        axis=1,
+    )
+    query_rows, output_rows = draft_the_tasks(
+        query_projection_weight, state=output_projection_weight
+    )
     row_ids = iota((group_blocks, width), 1)
     live = one_hot(row_ids < block_fill[:, None]).reshape(tokens, 1)
     query_masked = query_cotangent * live

time: 493 us -> 478 us (0.970)
  waiting for transfers between devices: 344 us -> 323 us
    all_gather x2 -> x1, waiting for transfers between devices: 104 us -> 83.1 us  [on_device(): lax.all_gather(jnp.concatenate([block_here, state], axis=1), 'near', axis...]
    all_gather x1, waiting for transfers between devices: 5.13 us -> 0.01 us  [on_device(): att_full = lax.all_gather(attended, 'mp', axis=1, tiled=True)]
  transfers between devices with their start and end apart: 15 -> 14, of which waited for: 9 -> 8; matrix products, arithmetic and copies ran while one was open for 16% -> 18% of each run, Pallas kernels for 0% -> 0%
where the time goes in v1:
time: 478 us; the launch traced here: 477 us
  waiting for transfers between devices  323 us (68%)
  matrix products  51.8 us (11%)
  starting transfers between devices  47.7 us (10%)
  other arithmetic  27.9 us (6%)
  between operations  14.5 us (3%)
  local copies, waits for them, and re-layouts  8.29 us (2%)
    all_to_all x7, waiting for transfers between devices, exchange(): return lax.all_to_all(values, axis, split_axis=0, concat_axis=0, tiled=True)  179 us
    all_gather x1, waiting for transfers between devices, on_device(): lax.all_gather(jnp.concatenate([block_here, state], axis=1), 'near', axis...  83.1 us
    all_gather x2, waiting for transfers between devices, on_device(): lax.all_gather(masked, 'far', axis=0, tiled=True)  56.3 us
    dot_general x30, matrix products, product(): lax.dot_general(left, right, ((contract[:1], contract[1:]), ((), ())), pr...  51.8 us
    all_to_all x7, starting transfers between devices, exchange(): return lax.all_to_all(values, axis, split_axis=0, concat_axis=0, tiled=True)  47.2 us
    concatenate x1, other arithmetic, on_device(): jnp.concatenate([stacked_columns(hid_full, far), stacked_columns(att_full...  13.9 us
  transfers between devices with their start and end apart: 14, of which 8 were waited for; matrix products, arithmetic and copies ran while one was open for 18% of the time, Pallas kernels for 0%

profile of v1, /device:TPU:12, one launch (start us, length us, event | category | flops | bytes accessed | tf_op | source)
XLA Modules:
  0.0 476.8 jit_solution(15776530752277415124)
XLA Ops:
  11.8 2.9 pad_maximum_fusion
  19.1 7.2 %all-to-all-start.2 = ((bf16[16,8,8320]{2,1,0:T(8,128)(2,1)}), bf16[16,8,8320]{2,1,0:T(8,128)(2,1)S(1)}, u32[]{:S(2)}, u32[]{:S(2)}) async-start(bf16[16,8,8320]{2,1,0:T(8,128)(2,1)} %bitcast.69), calls=%async_computation.2 | async-start | bytes 4259840 | tf_op jit(solution)/shard_map/all_to_all | solution.py:34
  28.4 3.4 all-gather.6.cloned.1.call-done
  33.2 13.9 %maximum_maximum_fusion = bf16[512,2048]{1,0:T(8,128)(2,1)} fusion(bf16[128,1024]{1,0:T(8,128)(2,1)S(1)} %copy-done.10, bf16[128,1024]{1,0:T(8,128)(2,1)S(1)} %copy-done.11, bf16[128,1024]{1,0:T(8,128)(2,1)S(1)} %copy-done.12, bf16[128,1024]{1,0:T(8,128)(2,1)S(1)} %get-tuple-element.20, bf16[128,1024]{1,0:T(8,128)(2,1)S(1)} %get-tuple-element.17, ...), kind=kLoop, calls=%fused_computation.40 | loop fusion | flops 16777216 | bytes 4194304 | tf_op jit(solution)/shard_map/concatenate | solution.py:138
  47.1 61.7 %all-to-all-done.2 = bf16[16,8,8320]{2,1,0:T(8,128)(2,1)S(1)} async-done(((bf16[16,8,8320]{2,1,0:T(8,128)(2,1)}), bf16[16,8,8320]{2,1,0:T(8,128)(2,1)S(1)}, u32[]{:S(2)}, u32[]{:S(2)}) %all-to-all-start.2) | async-done | bytes 2129952 | tf_op jit(solution)/shard_map/all_to_all | solution.py:34
  108.8 4.5 all-to-all-start
  113.9 83.1 %all-gather.10.cloned.1.call-done = bf16[1024,4096]{1,0:T(8,128)(2,1)} async-done(((bf16[256,4096]{1,0:T(8,128)(2,1)}), bf16[1024,4096]{1,0:T(8,128)(2,1)}) %all-gather.10.cloned.1.call-update) | async-done | bytes 8388624 | tf_op jit(solution)/shard_map/all_gather | solution.py:61
  196.9 6.2 %fusion.26 = bf16[512,1024]{1,0:T(8,128)(2,1)} fusion(bf16[512,2048]{1,0:T(8,128)(2,1)} %all-gather.12.cloned.1.call-done, bf16[1024,4096]{1,0:T(8,128)(2,1)} %all-gather.10.cloned.1.call-done), kind=kOutput, calls=%fused_computation.43 | convolution fusion | flops 2148007936 | bytes 7340032 | tf_op jit(solution)/shard_map/dot_general | solution.py:10
  203.1 5.1 %all-to-all-start.5 = ((bf16[4,128,1024]{2,1,0:T(8,128)(2,1)}), bf16[4,128,1024]{2,1,0:T(8,128)(2,1)}, u32[]{:S(2)}, u32[]{:S(2)}) async-start(bf16[4,128,1024]{2,1,0:T(8,128)(2,1)} %bitcast.82), calls=%async_computation.5 | async-start | bytes 2097152 | tf_op jit(solution)/shard_map/all_to_all | solution.py:34
  208.2 56.3 %all-gather.14.cloned.1.call-done = bf16[512,2048]{1,0:T(8,128)(2,1)} async-done(((bf16[128,2048]{1,0:T(8,128)(2,1)}), bf16[512,2048]{1,0:T(8,128)(2,1)}) %all-gather.14.cloned.1.call-update) | async-done | bytes 2097168 | tf_op jit(solution)/shard_map/all_gather | solution.py:142
  264.5 6.2 %fusion.29 = bf16[512,1024]{1,0:T(8,128)(2,1)} fusion(bf16[512,2048]{1,0:T(8,128)(2,1)} %all-gather.14.cloned.1.call-done, bf16[1024,4096]{1,0:T(8,128)(2,1)} %all-gather.10.cloned.1.call-done), kind=kOutput, calls=%fused_computation.44 | convolution fusion | flops 2148007936 | bytes 7340032 | tf_op jit(solution)/shard_map/dot_general | solution.py:10
  270.7 7.3 %all-to-all-start.6 = ((bf16[4,128,1024]{2,1,0:T(8,128)(2,1)}), bf16[4,128,1024]{2,1,0:T(8,128)(2,1)}, u32[]{:S(2)}, u32[]{:S(2)}) async-start(bf16[4,128,1024]{2,1,0:T(8,128)(2,1)} %bitcast.83), calls=%async_computation.7 | async-start | bytes 2097152 | tf_op jit(solution)/shard_map/all_to_all | solution.py:34
  278.0 6.2 %fusion.8 = bf16[512,2048]{1,0:T(8,128)(2,1)} fusion(bf16[1024,4096]{1,0:T(8,128)(2,1)} %all-gather.10.cloned.1.call-done, bf16[512,2048]{1,0:T(8,128)(2,1)} %bitcast.1), kind=kOutput, calls=%fused_computation.10 | convolution fusion | flops 2148532224 | bytes 7340032 | tf_op jit(solution)/shard_map/dot_general | solution.py:10
  284.2 16.6 %all-to-all-done.6 = bf16[4,128,1024]{2,1,0:T(8,128)(2,1)} async-done(((bf16[4,128,1024]{2,1,0:T(8,128)(2,1)}), bf16[4,128,1024]{2,1,0:T(8,128)(2,1)}, u32[]{:S(2)}, u32[]{:S(2)}) %all-to-all-start.6) | async-done | bytes 1048608 | tf_op jit(solution)/shard_map/all_to_all | solution.py:34
  300.7 7.8 %all-to-all-start.1 = ((bf16[4,128,2048]{2,1,0:T(8,128)(2,1)}), bf16[4,128,2048]{2,1,0:T(8,128)(2,1)}, u32[]{:S(2)}, u32[]{:S(2)}) async-start(bf16[4,128,2048]{2,1,0:T(8,128)(2,1)} %bitcast.75), calls=%async_computation.1 | async-start | bytes 4194304 | tf_op jit(solution)/shard_map/all_to_all | solution.py:34
  313.0 6.2 %fusion.11 = bf16[512,2048]{1,0:T(8,128)(2,1)} fusion(bf16[1024,4096]{1,0:T(8,128)(2,1)} %all-gather.10.cloned.1.call-done, bf16[512,2048]{1,0:T(8,128)(2,1)} %bitcast.1), kind=kOutput, calls=%fused_computation.11 | convolution fusion | flops 2148532224 | bytes 7340032 | tf_op jit(solution)/shard_map/dot_general | solution.py:10
  319.2 33.8 %all-to-all-done.1 = bf16[4,128,2048]{2,1,0:T(8,128)(2,1)} async-done(((bf16[4,128,2048]{2,1,0:T(8,128)(2,1)}), bf16[4,128,2048]{2,1,0:T(8,128)(2,1)}, u32[]{:S(2)}, u32[]{:S(2)}) %all-to-all-start.1) | async-done | bytes 2097184 | tf_op jit(solution)/shard_map/all_to_all | solution.py:34
  353.0 7.8 %all-to-all-start.4 = ((bf16[4,128,2048]{2,1,0:T(8,128)(2,1)}), bf16[4,128,2048]{2,1,0:T(8,128)(2,1)}, u32[]{:S(2)}, u32[]{:S(2)}) async-start(bf16[4,128,2048]{2,1,0:T(8,128)(2,1)} %bitcast.74), calls=%async_computation.4 | async-start | bytes 4194304 | tf_op jit(solution)/shard_map/all_to_all | solution.py:34
  362.7 3.4 psum.7
  370.5 34.8 %all-to-all-done.4 = bf16[4,128,2048]{2,1,0:T(8,128)(2,1)} async-done(((bf16[4,128,2048]{2,1,0:T(8,128)(2,1)}), bf16[4,128,2048]{2,1,0:T(8,128)(2,1)}, u32[]{:S(2)}, u32[]{:S(2)}) %all-to-all-start.4) | async-done | bytes 2097184 | tf_op jit(solution)/shard_map/all_to_all | solution.py:34
  405.3 7.6 %all-to-all-start.3 = ((bf16[16,8,8192]{2,1,0:T(8,128)(2,1)}), bf16[16,8,8192]{2,1,0:T(8,128)(2,1)}, u32[]{:S(2)}, u32[]{:S(2)}) async-start(bf16[16,8,8192]{2,1,0:T(8,128)(2,1)} %maximum_bitcast_fusion), calls=%async_computation.3 | async-start | bytes 4194304 | tf_op jit(solution)/shard_map/all_to_all | solution.py:34
  429.3 31.6 %all-to-all-done.3 = bf16[16,8,8192]{2,1,0:T(8,128)(2,1)} async-done(((bf16[16,8,8192]{2,1,0:T(8,128)(2,1)}), bf16[16,8,8192]{2,1,0:T(8,128)(2,1)}, u32[]{:S(2)}, u32[]{:S(2)}) %all-to-all-start.3) | async-done | bytes 2097184 | tf_op jit(solution)/shard_map/all_to_all | solution.py:34
  465.3 2.3 fusion.20
  467.6 2.3 fusion.21
  (102 shorter events, 44.4 us)
Async XLA Ops:
  7.2 305.2 %copy-start = (bf16[16,16,2048]{2,1,0:T(8,128)(2,1)S(1)}, bf16[16,16,2048]{2,1,0:T(8,128)(2,1)}, u32[]{:S(2)}) copy-start(bf16[16,16,2048]{2,1,0:T(8,128)(2,1)} %param.20) | copy-start | bytes 3145732
  7.2 4.6 copy-start.9
  7.2 19.1 %all-gather.8.cloned.1.call-start = ((), (), s32[]{:S(2)}) async-start(), calls=%async_computation.10 | async-start | bytes 1572864 | tf_op jit(solution)/shard_map/all_gather | solution.py:135
  7.9 23.8 %all-gather.6.cloned.1.call-start = ((), (), s32[]{:S(2)}) async-start(), calls=%async_computation.9 | async-start | bytes 1572864 | tf_op jit(solution)/shard_map/all_gather | solution.py:134
  8.7 105.2 %all-gather.12.cloned.1.call-start = ((), (), s32[]{:S(2)}) async-start(), calls=%async_computation.12 | async-start | bytes 2621440 | tf_op jit(solution)/shard_map/all_gather | solution.py:142
  11.7 6.3 %copy-start.1 = (bf16[128,2048]{1,0:T(8,128)(2,1)}, bf16[128,2048]{1,0:T(8,128)(2,1)S(1)}, u32[]{:S(2)}) copy-start(bf16[128,2048]{1,0:T(8,128)(2,1)S(1)} %get-tuple-element.24) | copy-start | bytes 1572868
  11.7 3.0 copy-start.15
  11.7 185.2 %all-gather.10.cloned.1.call-start = ((), (), s32[]{:S(2)}) async-start(), calls=%async_computation.11 | async-start | bytes 10485760 | tf_op jit(solution)/shard_map/all_gather | solution.py:61
  14.7 1.7 copy-start.2
  19.1 89.6 %all-to-all-start.2 = ((bf16[16,8,8320]{2,1,0:T(8,128)(2,1)}), bf16[16,8,8320]{2,1,0:T(8,128)(2,1)S(1)}, u32[]{:S(2)}, u32[]{:S(2)}) async-start(bf16[16,8,8320]{2,1,0:T(8,128)(2,1)} %bitcast.69), calls=%async_computation.2 | async-start | bytes 4259840 | tf_op jit(solution)/shard_map/all_to_all | solution.py:34
  31.8 1.4 copy-start.12
  108.8 94.3 %all-to-all-start = ((bf16[4,128,2048]{2,1,0:T(8,128)(2,1)}), bf16[4,128,2048]{2,1,0:T(8,128)(2,1)}, u32[]{:S(2)}, u32[]{:S(2)}) async-start(bf16[4,128,2048]{2,1,0:T(8,128)(2,1)} %bitcast.68), calls=%async_computation | async-start | bytes 4194304 | tf_op jit(solution)/shard_map/all_to_all | solution.py:34
  113.3 151.3 %all-gather.14.cloned.1.call-start = ((), (), s32[]{:S(2)}) async-start(), calls=%async_computation.14 | async-start | bytes 2621440 | tf_op jit(solution)/shard_map/all_gather | solution.py:142
  203.1 67.6 %all-to-all-start.5 = ((bf16[4,128,1024]{2,1,0:T(8,128)(2,1)}), bf16[4,128,1024]{2,1,0:T(8,128)(2,1)}, u32[]{:S(2)}, u32[]{:S(2)}) async-start(bf16[4,128,1024]{2,1,0:T(8,128)(2,1)} %bitcast.82), calls=%async_computation.5 | async-start | bytes 2097152 | tf_op jit(solution)/shard_map/all_to_all | solution.py:34
  270.7 30.0 %all-to-all-start.6 = ((bf16[4,128,1024]{2,1,0:T(8,128)(2,1)}), bf16[4,128,1024]{2,1,0:T(8,128)(2,1)}, u32[]{:S(2)}, u32[]{:S(2)}) async-start(bf16[4,128,1024]{2,1,0:T(8,128)(2,1)} %bitcast.83), calls=%async_computation.7 | async-start | bytes 2097152 | tf_op jit(solution)/shard_map/all_to_all | solution.py:34
  300.7 52.3 %all-to-all-start.1 = ((bf16[4,128,2048]{2,1,0:T(8,128)(2,1)}), bf16[4,128,2048]{2,1,0:T(8,128)(2,1)}, u32[]{:S(2)}, u32[]{:S(2)}) async-start(bf16[4,128,2048]{2,1,0:T(8,128)(2,1)} %bitcast.75), calls=%async_computation.1 | async-start | bytes 4194304 | tf_op jit(solution)/shard_map/all_to_all | solution.py:34
  353.0 52.3 %all-to-all-start.4 = ((bf16[4,128,2048]{2,1,0:T(8,128)(2,1)}), bf16[4,128,2048]{2,1,0:T(8,128)(2,1)}, u32[]{:S(2)}, u32[]{:S(2)}) async-start(bf16[4,128,2048]{2,1,0:T(8,128)(2,1)} %bitcast.74), calls=%async_computation.4 | async-start | bytes 4194304 | tf_op jit(solution)/shard_map/all_to_all | solution.py:34
  366.0 1.6 copy-start.6
  366.0 2.0 copy-start.7
  366.7 1.6 copy-start.13
  405.3 55.6 %all-to-all-start.3 = ((bf16[16,8,8192]{2,1,0:T(8,128)(2,1)}), bf16[16,8,8192]{2,1,0:T(8,128)(2,1)}, u32[]{:S(2)}, u32[]{:S(2)}) async-start(bf16[16,8,8192]{2,1,0:T(8,128)(2,1)} %maximum_bitcast_fusion), calls=%async_computation.3 | async-start | bytes 4194304 | tf_op jit(solution)/shard_map/all_to_all | solution.py:34
  412.9 2.7 copy-start.14
  412.9 52.4 %reduce-scatter.3.cloned.1.call-start = ((), (), s32[]{:S(2)}) async-start(), calls=%async_computation.13 | async-start | bytes 1572864 | tf_op jit(solution)/shard_map/reduce_scatter | solution.py:154
  415.3 52.4 %reduce-scatter.5.cloned.1.call-start = ((), (), s32[]{:S(2)}) async-start(), calls=%async_computation.15 | async-start | bytes 1572864 | tf_op jit(solution)/shard_map/reduce_scatter | solution.py:154
  (6 other events, 7.7 us)
Sparse Core Ops, SparseCore 0:
  9.5 10.3 all-gather.7
  21.5 10.2 all-gather.5
  33.9 70.9 all-gather.11
  107.2 89.6 all-gather.9
  198.9 65.5 all-gather.13
  415.6 9.5 reduce-scatter.2
  427.5 9.5 reduce-scatter.4
